TPU v7x, 32 devices: a whole 2x2x4 slice. The times are simulated.
32 devices in a mesh: dp: 2 (over x), ctx: 16 (over z, y, core).
Axes of the slice: x: 2, y: 2, z: 4, core: 2. Of those that a mesh axis runs over, the one named last changes fastest.
Arguments:
- features: bfloat16 [2, 2048, 1024], P('dp', 'ctx'), may hold values from -6 to 6
- gate_in: bfloat16 [2, 2048, 1024], P('dp', 'ctx'), may hold values from -6 to 6
- state_in: bfloat16 [2, 2048, 64], P('dp', 'ctx'), may hold values from -0.59765625 to 0.59765625
- state_out: bfloat16 [2, 2048, 64], P('dp', 'ctx'), may hold values from -0.59765625 to 0.59765625
- step_size: float32 [2, 8, 2048], P('dp', None, 'ctx'), may hold values from 0 to 4096
- decay_rate: float32 [8], replicated, may hold values from 0 to 1
- user_ids: int32 [2, 2048], P('dp', 'ctx'), may hold values from 0 to 3, never falling along the last dimension, each value on 1 to 1024 neighbouring positions
- norm_gain: bfloat16 [1024], replicated, may hold values from 0.099609375 to 1.8984375
- out_weight: bfloat16 [1024, 512], P(('dp', 'ctx')), may hold values from -0.1875 to 0.1875
- out_grad: bfloat16 [2, 2048, 512], P('dp', 'ctx'), may hold values from -6 to 6
Outputs:
- mixed: bfloat16 [2, 2048, 512], P('dp', 'ctx')
- feature_grad: bfloat16 [2, 2048, 1024], P('dp', 'ctx')
- weight_grad: float32 [1024, 512], P(('dp', 'ctx'))
Inputs may be any that keep to these rules, and one draw needn't show every extreme that they name: `user_ids`: each of the 4 users of a history holds consecutive events; ids never fall along a history, and one user holds exactly 1024 events.
All inputs are finite; a program needn't handle non-finite values.
Results may differ from a plain program's by a relative error of at most 0.019.
Values may be sent and summed in bfloat16 or wider, within the bound.
A program may use at most 64 MiB of HBM per device.

v0:
```python
import jax
import jax.numpy as jnp
from jax import lax
from jax.sharding import PartitionSpec as P

eps = 1e-05


def carried_in(value, axis, join, neutral, backward):
    count, mine = (lax.axis_size(axis), lax.axis_index(axis))
    pieces = jax.tree.map(lambda part: lax.all_gather(part, axis), value)
    if backward:
        pieces = jax.tree.map(lambda part: part[::-1], pieces)
        mine = count - 1 - mine
    running = jax.tree.map(
        lambda part, zero: jnp.full_like(part, 0) + jnp.asarray(zero, part.dtype), value, neutral
    )

    def step(position, running):
        longer = join(running, jax.tree.map(lambda part: part[position], pieces))
        return jax.tree.map(lambda new, old: jnp.where(position < mine, new, old), longer, running)

    return lax.fori_loop(0, count - 1, step, running)


def padded(x, sides, width):
    for axis, dim in sides:
        size, length = (lax.axis_size(axis), x.shape[dim])
        up = [(i, (i + 1) % size) for i in range(size - 1)]
        down = [(j, i) for i, j in up]
        last = lax.slice_in_dim(x, length - width, length, axis=dim)
        leading = lax.slice_in_dim(x, 0, width, axis=dim)
        before = lax.ppermute(last, axis, up)
        after = lax.ppermute(leading, axis, down)
        x = jnp.concatenate([before, x, after], axis=dim)
    return x


def carry_combine(earlier, following):
    gain_out = (earlier[0].astype(jnp.float32) * following[0].astype(jnp.float32)).astype(
        jnp.bfloat16
    )
    state_out = (
        following[0].astype(jnp.float32)[:, None, None] * earlier[1].astype(jnp.float32)
        + following[1].astype(jnp.float32)
    ).astype(jnp.bfloat16)
    return (gain_out, state_out)


def block_terms(values, keys_in, reads, logdec, user_row, before_user, after_user):
    row_count = values.shape[0]
    head_count = logdec.shape[0]
    cumulative = jnp.cumsum(logdec, axis=1)
    total_log = cumulative[:, -1]
    intersections = jnp.dot(reads, keys_in.T, preferred_element_type=jnp.float32)
    same_user = user_row[:, None] == user_row[None, :]
    spread = cumulative[:, :, None] - cumulative[:, None, :]
    doubled = 1.0 + jnp.eye(row_count, dtype=jnp.float32)
    weights = jnp.where(
        same_user[None], intersections[None] * doubled[None] * jnp.exp(-jnp.abs(spread)), 0.0
    ).astype(jnp.bfloat16)
    per_head = values.reshape(row_count, head_count, -1)
    inner = jnp.einsum("hts,shp->thp", weights, per_head, preferred_element_type=jnp.float32)
    tail_user = (user_row == user_row[-1]).astype(jnp.float32)
    head_user = (user_row == user_row[0]).astype(jnp.float32)
    fwd_scale = (jnp.exp(total_log[:, None] - cumulative) * tail_user[None]).T
    rev_scale = (jnp.exp(cumulative) * head_user[None]).T
    fwd_keys = (keys_in[:, None, :] * fwd_scale[:, :, None]).astype(jnp.bfloat16)
    rev_keys = (keys_in[:, None, :] * rev_scale[:, :, None]).astype(jnp.bfloat16)
    fwd_state = jnp.einsum(
        "shn,shp->hnp", fwd_keys, per_head, preferred_element_type=jnp.float32
    ).astype(jnp.bfloat16)
    rev_state = jnp.einsum(
        "shn,shp->hnp", rev_keys, per_head, preferred_element_type=jnp.float32
    ).astype(jnp.bfloat16)
    passing = jnp.exp(total_log)
    fwd_gain = (passing * (user_row[-1] == before_user).astype(jnp.float32)).astype(jnp.bfloat16)
    rev_gain = (passing * (user_row[0] == after_user).astype(jnp.float32)).astype(jnp.bfloat16)
    return (inner, cumulative, fwd_gain, fwd_state, rev_gain, rev_state)


def apply_carries(
    inner, reads, cumulative, user_row, before_user, after_user, from_before, from_after
):
    earlier_part = jnp.einsum("tn,hnp->thp", reads, from_before, preferred_element_type=jnp.float32)
    following_part = jnp.einsum(
        "tn,hnp->thp", reads, from_after, preferred_element_type=jnp.float32
    )
    earlier_scale = (jnp.exp(cumulative) * (user_row == before_user).astype(jnp.float32)[None]).T[
        :, :, None
    ]
    following_scale = (
        jnp.exp(cumulative[:, -1:] - cumulative)
        * (user_row == after_user).astype(jnp.float32)[None]
    ).T[:, :, None]
    row_count = inner.shape[0]
    return (inner + earlier_scale * earlier_part + following_scale * following_part).reshape(
        row_count, -1
    )


def mix_local(values, keys_in, reads, logdec, user_row, before_user, after_user):
    inner, cumulative, fwd_gain, fwd_state, rev_gain, rev_state = block_terms(
        values, keys_in, reads, logdec, user_row, before_user, after_user
    )
    neutral = jnp.ones_like(fwd_gain)
    nothing = jnp.zeros_like(fwd_state)
    from_before = carried_in(
        (fwd_gain, fwd_state), "ctx", carry_combine, (neutral, nothing), False
    )[1]
    from_after = carried_in((rev_gain, rev_state), "ctx", carry_combine, (neutral, nothing), True)[
        1
    ]
    return apply_carries(
        inner, reads, cumulative, user_row, before_user, after_user, from_before, from_after
    )


def local(
    features,
    gate_in,
    state_in,
    state_out,
    step_size,
    decay_rate,
    user_ids,
    norm_gain,
    out_weight,
    out_grad,
):
    neighbours = padded(user_ids + 1, (("ctx", 1),), 1) - 1
    user_row = user_ids[0]
    before_user = neighbours[0, 0]
    after_user = neighbours[0, -1]
    logdec = -step_size[0] * decay_rate[:, None]
    values = features[0]
    gates = gate_in[0]
    keys_in = state_in[0]
    reads = state_out[0]
    grad_local = out_grad[0]
    mixed_wide = mix_local(values, keys_in, reads, logdec, user_row, before_user, after_user)

    def normalize(mixed_rows):
        gated = mixed_rows * jax.nn.silu(gates.astype(jnp.float32))
        multiplier_value = lax.rsqrt(jnp.mean(gated * gated, axis=-1, keepdims=True) + eps)
        return gated * multiplier_value * norm_gain.astype(jnp.float32)

    normed_wide, pullback = jax.vjp(normalize, mixed_wide)
    normed_out = normed_wide.astype(jnp.bfloat16)
    full_weight = lax.all_gather(out_weight, ("dp", "ctx"), axis=0, tiled=True)
    result = jnp.dot(normed_out, full_weight, preferred_element_type=jnp.float32)
    grad_normed = lax.dot_general(
        grad_local, full_weight, (((1,), (1,)), ((), ())), preferred_element_type=jnp.float32
    )
    grad_mixed = pullback(grad_normed)[0].astype(jnp.bfloat16)
    grad_feat = mix_local(grad_mixed, reads, keys_in, logdec, user_row, before_user, after_user)
    weight_grad = lax.psum_scatter(
        lax.dot_general(
            normed_out, grad_local, (((0,), (0,)), ((), ())), preferred_element_type=jnp.float32
        ),
        ("dp", "ctx"),
        scatter_dimension=0,
        tiled=True,
    )
    return (result.astype(jnp.bfloat16)[None], grad_feat.astype(jnp.bfloat16)[None], weight_grad)


def solution(mesh):
    placed = (
        P("dp", "ctx", None),
        P("dp", "ctx", None),
        P("dp", "ctx", None),
        P("dp", "ctx", None),
        P("dp", None, "ctx"),
        P(),
        P("dp", "ctx"),
        P(),
        P(("dp", "ctx"), None),
        P("dp", "ctx", None),
    )
    return jax.shard_map(
        local,
        mesh=mesh,
        in_specs=placed,
        out_specs=(P("dp", "ctx", None), P("dp", "ctx", None), P(("dp", "ctx"), None)),
        check_vma=False,
    )
```

profile of v0, /device:TPU:0, one launch (start us, length us, event | category | flops | bytes accessed | tf_op | source)
XLA Modules:
  0.0 398.8 jit_solution(13853915928123735821)
XLA Ops:
  8.6 2.8 collective-permute-start
  11.4 1.3 collective-permute-start.1
  12.7 1.3 fusion.76
  17.0 1.3 add_add_fusion.1
  19.0 3.2 fusion.67
  25.5 1.6 convolution_multiply_fusion.2
  27.1 1.3 bitcast_convert_fusion.5
  28.4 1.4 broadcast_compare_fusion
  34.9 36.1 %all-reduce.2 = (bf16[128]{0:T(256)(128)(2,1)S(1)}, bf16[128]{0:T(256)(128)(2,1)S(1)}) all-reduce(bf16[128]{0:T(256)(128)(2,1)S(1)} %dynamic-update-slice.1, bf16[128]{0:T(256)(128)(2,1)S(1)} %dynamic-update-slice), channel_id=4, replica_groups=mesh['dp'=2,'ctx'=16] {'ctx'}, use_global_device_ids=true, to_apply=%add.1 | all-reduce | flops 256 | bytes 1024
  72.4 1.8 rev.11
  74.2 29.6 %while.57 = (s32[]{:T(128)}, bf16[8,64,128]{2,1,0:T(8,128)(2,1)S(1)}, s32[]{:T(128)}, bf16[16,8]{1,0:T(8,128)(2,1)}, bf16[16,8,64,128]{3,2,1,0:T(8,128)(2,1)S(1)}, /*index=5*/s32[]{:T(128)}, s32[]{:T(128)}) while((s32[]{:T(128)}, bf16[8,64,128]{2,1,0:T(8,128)(2,1)S(1)}, s32[]{:T(128)}, bf16[16,8]{1,0:T(8,128)(2,1)}, ...), condition=%wide.region_4.5_spmd.clone, body=%wide.region_3.4_spmd.clone.sunk | while | flops 458764 | bytes 393401 | solution.py:23
  76.2 1.2 bitcast_convert_fusion.11
  78.1 1.2 bitcast_convert_fusion.11
  89.9 1.2 bitcast_convert_fusion.11
  91.9 1.2 bitcast_convert_fusion.11
  93.9 1.2 bitcast_convert_fusion.11
  95.8 1.2 bitcast_convert_fusion.11
  97.8 1.2 bitcast_convert_fusion.11
  99.8 1.2 bitcast_convert_fusion.11
  101.8 1.2 bitcast_convert_fusion.11
  103.8 8.7 %all-gather.14.cloned.1.call-done = bf16[128,64,128]{2,1,0:T(8,128)(2,1)} async-done(((bf16[8,64,128]{2,1,0:T(8,128)(2,1)}), bf16[128,64,128]{2,1,0:T(8,128)(2,1)}) %all-gather.14.cloned.1.call-update) | async-done | bytes 2097168 | tf_op jit(solution)/shard_map/all_gather | solution.py:11
  112.5 25.8 %while.56 = (s32[]{:T(128)}, bf16[8,64,128]{2,1,0:T(8,128)(2,1)S(1)}, s32[]{:T(128)}, bf16[16,8]{1,0:T(8,128)(2,1)}, bf16[16,8,64,128]{3,2,1,0:T(8,128)(2,1)}, /*index=5*/s32[]{:T(128)}, s32[]{:T(128)}) while((s32[]{:T(128)}, bf16[8,64,128]{2,1,0:T(8,128)(2,1)S(1)}, s32[]{:T(128)}, bf16[16,8]{1,0:T(8,128)(2,1)}, ...), condition=%wide.region_2.3_spmd.clone, body=%wide.region_1.2_spmd.clone.sunk | while | flops 458764 | bytes 393401 | solution.py:23
  139.6 28.4 %all-gather.12.cloned.1.call-done = bf16[1024,512]{1,0:T(8,128)(2,1)} async-done(((bf16[32,512]{1,0:T(8,128)(2,1)}), bf16[1024,512]{1,0:T(8,128)(2,1)}) %all-gather.12.cloned.1.call-update) | async-done | bytes 1048592 | tf_op jit(solution)/shard_map/all_gather | solution.py:150
  168.0 1.8 multiply_reduce_fusion
  173.1 1.7 fusion.45
  174.9 2.3 fusion.17
  177.2 34.3 %all-gather.20.cloned.1.call-done = bf16[128,64,128]{2,1,0:T(8,128)(2,1)} async-done(((bf16[8,64,128]{2,1,0:T(8,128)(2,1)}), bf16[128,64,128]{2,1,0:T(8,128)(2,1)}) %all-gather.20.cloned.1.call-update) | async-done | bytes 2097168 | tf_op jit(solution)/shard_map/all_gather | solution.py:11
  211.5 1.8 rev.12
  213.3 12.1 %while.59 = (s32[]{:T(128)}, bf16[8,64,128]{2,1,0:T(8,128)(2,1)S(1)}, s32[]{:T(128)}, bf16[16,8]{1,0:T(8,128)(2,1)}, bf16[16,8,64,128]{3,2,1,0:T(8,128)(2,1)S(1)}, /*index=5*/s32[]{:T(128)}, s32[]{:T(128)}) while((s32[]{:T(128)}, bf16[8,64,128]{2,1,0:T(8,128)(2,1)S(1)}, s32[]{:T(128)}, bf16[16,8]{1,0:T(8,128)(2,1)}, ...), condition=%wide.region_10.11_spmd.clone, body=%wide.region_9.10_spmd.clone.sunk | while | flops 458764 | bytes 393401 | solution.py:23
  225.8 27.9 %all-gather.18.cloned.1.call-done = bf16[128,64,128]{2,1,0:T(8,128)(2,1)} async-done(((bf16[8,64,128]{2,1,0:T(8,128)(2,1)}), bf16[128,64,128]{2,1,0:T(8,128)(2,1)}) %all-gather.18.cloned.1.call-update) | async-done | bytes 2097168 | tf_op jit(solution)/shard_map/all_gather | solution.py:11
  253.7 25.8 %while.58 = (s32[]{:T(128)}, bf16[8,64,128]{2,1,0:T(8,128)(2,1)S(1)}, s32[]{:T(128)}, bf16[16,8]{1,0:T(8,128)(2,1)}, bf16[16,8,64,128]{3,2,1,0:T(8,128)(2,1)}, /*index=5*/s32[]{:T(128)}, s32[]{:T(128)}) while((s32[]{:T(128)}, bf16[8,64,128]{2,1,0:T(8,128)(2,1)S(1)}, s32[]{:T(128)}, bf16[16,8]{1,0:T(8,128)(2,1)}, ...), condition=%wide.region_8.9_spmd.clone, body=%wide.region_7.8_spmd.clone.sunk | while | flops 458764 | bytes 393401 | solution.py:23
  281.1 110.8 %reduce-scatter.2.cloned.1.call-done = f32[32,512]{1,0:T(8,128)} async-done(((f32[1024,512]{1,0:T(8,128)}), f32[32,512]{1,0:T(8,128)}) %reduce-scatter.2.cloned.1.call-update) | async-done | bytes 65552 | tf_op jit(solution)/shard_map/reduce_scatter | solution.py:157
  (216 shorter events, 99.7 us)
Async XLA Ops:
  7.2 160.9 %copy-start = (bf16[1,128,512]{2,1,0:T(8,128)(2,1)S(1)}, bf16[1,128,512]{2,1,0:T(8,128)(2,1)}, u32[]{:S(2)}) copy-start(bf16[1,128,512]{2,1,0:T(8,128)(2,1)} %param.27) | copy-start | bytes 393220
  7.2 23.4 %copy-start.24 = (u32[32]{0:T(128)S(1)}, u32[32]{0:T(128)}, u32[]{:S(2)}) copy-start(u32[32]{0:T(128)} %constant.130) | copy-start | bytes 388
  7.2 22.6 %copy-start.1 = (bf16[1,128,1024]{2,1,0:T(8,128)(2,1)S(1)}, bf16[1,128,1024]{2,1,0:T(8,128)(2,1)}, u32[]{:S(2)}) copy-start(bf16[1,128,1024]{2,1,0:T(8,128)(2,1)} %param.19) | copy-start | bytes 786436
  7.2 22.7 %copy-start.23 = (bf16[1024]{0:T(1024)(128)(2,1)S(1)}, bf16[1024]{0:T(1024)(128)(2,1)}, u32[]{:S(2)}) copy-start(bf16[1024]{0:T(1024)(128)(2,1)} %param.25) | copy-start | bytes 6148
  7.2 65.2 %all-gather.16.cloned.1.call-start = ((), (), s32[]{:S(2)}) async-start(), calls=%async_computation.4 | async-start | bytes 2228224 | tf_op jit(solution)/shard_map/all_gather | solution.py:11
  8.6 8.4 %collective-permute-start = (s32[1,1]{1,0:T(1,128)}, s32[1,1]{1,0:T(1,128)}, u32[]{:S(2)}, u32[]{:S(2)}) collective-permute-start(s32[1,1]{1,0:T(1,128)} %get-tuple-element.528), channel_id=1, source_target_pairs={{0,1},{1,2},{2,3},{3,4},{4,5},{5,6},{6,7},{7,8},{8,9},{9,10},{10,1... | collective-permute-start | bytes 20 | tf_op jit(solution)/shard_map/ppermute | solution.py:33
  11.4 5.6 %collective-permute-start.1 = (s32[1,1]{1,0:T(1,128)}, s32[1,1]{1,0:T(1,128)}, u32[]{:S(2)}, u32[]{:S(2)}) collective-permute-start(s32[1,1]{1,0:T(1,128)} %get-tuple-element.529), channel_id=1, source_target_pairs={{1,0},{2,1},{3,2},{4,3},{5,4},{6,5},{7,6},{8,7},{9,8},{10,9},{11,1... | collective-permute-start | bytes 20 | tf_op jit(solution)/shard_map/ppermute | solution.py:34
  15.1 57.3 %copy-start.7 = (f32[8,128]{1,0:T(8,128)}, f32[8,128]{1,0:T(8,128)S(1)}, u32[]{:S(2)}) copy-start(f32[8,128]{1,0:T(8,128)S(1)} %reduce_window_sum.12) | copy-start | bytes 12292
  22.8 2.6 copy-start.17
  22.8 2.6 copy-start.19
  23.7 88.8 %all-gather.14.cloned.1.call-start = ((), (), s32[]{:S(2)}) async-start(), calls=%async_computation.3 | async-start | bytes 2228224 | tf_op jit(solution)/shard_map/all_gather | solution.py:11
  24.7 143.4 %all-gather.12.cloned.1.call-start = ((), (), s32[]{:S(2)}) async-start(), calls=%async_computation.1 | async-start | bytes 1081344 | tf_op jit(solution)/shard_map/all_gather | solution.py:150
  25.4 186.1 %all-gather.20.cloned.1.call-start = ((), (), s32[]{:S(2)}) async-start(), calls=%async_computation.6 | async-start | bytes 2228224 | tf_op jit(solution)/shard_map/all_gather | solution.py:11
  74.2 64.1 %copy-start.2 = (bf16[1,128,64]{1,2,0:T(8,128)(2,1)S(1)}, bf16[1,128,64]{1,2,0:T(8,128)(2,1)}, u32[]{:S(2)}) copy-start(bf16[1,128,64]{1,2,0:T(8,128)(2,1)} %param.21) | copy-start | bytes 49156
  103.8 34.5 %copy-start.15 = (f32[128,8]{0,1:T(8,128)S(1)}, f32[128,8]{0,1:T(8,128)}, u32[]{:S(2)}) copy-start(f32[128,8]{0,1:T(8,128)} %get-tuple-element.514) | copy-start | bytes 12292
  103.8 34.8 %copy-start.13 = (f32[128,8]{0,1:T(8,128)S(1)}, f32[128,8]{0,1:T(8,128)}, u32[]{:S(2)}) copy-start(f32[128,8]{0,1:T(8,128)} %get-tuple-element.512) | copy-start | bytes 12292
  103.8 35.1 %copy-start.8 = (f32[8,128]{1,0:T(8,128)S(1)}, f32[8,128]{1,0:T(8,128)}, u32[]{:S(2)}) copy-start(f32[8,128]{1,0:T(8,128)} %copy-done.7) | copy-start | bytes 12292
  103.8 35.1 %copy-start.10 = (pred[128,128]{1,0:T(8,128)(4,1)S(1)}, pred[128,128]{1,0:T(8,128)(4,1)}, u32[]{:S(2)}) copy-start(pred[128,128]{1,0:T(8,128)(4,1)} %broadcast_compare_fusion) | copy-start | bytes 49156
  103.8 35.1 %copy-start.12 = (f32[128,128]{1,0:T(8,128)S(1)}, f32[128,128]{1,0:T(8,128)}, u32[]{:S(2)}) copy-start(f32[128,128]{1,0:T(8,128)} %convolution_multiply_fusion.2) | copy-start | bytes 196612
  138.9 29.1 %copy-start.22 = (f32[1024]{0:T(1024)S(1)}, f32[1024]{0:T(1024)}, u32[]{:S(2)}) copy-start(f32[1024]{0:T(1024)} %get-tuple-element.517) | copy-start | bytes 12292
  168.0 2.1 copy-start.20
  168.0 3.1 copy-start.18
  169.8 2.3 copy-start.3
  169.9 3.1 copy-start.21
  171.1 82.6 %all-gather.18.cloned.1.call-start = ((), (), s32[]{:S(2)}) async-start(), calls=%async_computation.5 | async-start | bytes 2228224 | tf_op jit(solution)/shard_map/all_gather | solution.py:11
  172.0 219.9 %reduce-scatter.2.cloned.1.call-start = ((), (), s32[]{:S(2)}) async-start(), calls=%async_computation.2 | async-start | bytes 2162688 | tf_op jit(solution)/shard_map/reduce_scatter | solution.py:157
  213.3 12.2 %copy-start.4 = (bf16[1,128,64]{1,2,0:T(8,128)(2,1)S(1)}, bf16[1,128,64]{1,2,0:T(8,128)(2,1)}, u32[]{:S(2)}) copy-start(bf16[1,128,64]{1,2,0:T(8,128)(2,1)} %param.20) | copy-start | bytes 49156
  213.3 12.2 %copy-start.16 = (f32[128,8]{0,1:T(8,128)S(1)}, f32[128,8]{0,1:T(8,128)}, u32[]{:S(2)}) copy-start(f32[128,8]{0,1:T(8,128)} %get-tuple-element.514) | copy-start | bytes 12292
  213.3 66.2 %copy-start.14 = (f32[128,8]{0,1:T(8,128)S(1)}, f32[128,8]{0,1:T(8,128)}, u32[]{:S(2)}) copy-start(f32[128,8]{0,1:T(8,128)} %get-tuple-element.512) | copy-start | bytes 12292
  225.5 54.3 %copy-start.6 = (f32[128,128]{1,0:T(8,128)S(1)}, f32[128,128]{1,0:T(8,128)}, u32[]{:S(2)}) copy-start(f32[128,128]{1,0:T(8,128)} %convolution_multiply_fusion.1) | copy-start | bytes 196612
  225.5 54.3 %copy-start.9 = (f32[8,128]{1,0:T(8,128)S(1)}, f32[8,128]{1,0:T(8,128)}, u32[]{:S(2)}) copy-start(f32[8,128]{1,0:T(8,128)} %copy-done.7) | copy-start | bytes 12292
  225.5 54.3 %copy-start.11 = (pred[128,128]{1,0:T(8,128)(4,1)S(1)}, pred[128,128]{1,0:T(8,128)(4,1)}, u32[]{:S(2)}) copy-start(pred[128,128]{1,0:T(8,128)(4,1)} %broadcast_compare_fusion) | copy-start | bytes 49156
  (1 other events, 2.1 us)
Sparse Core Ops, SparseCore 0:
  23.8 45.5 all-gather.15
  72.1 40.3 all-gather.13
  115.4 52.5 all-gather.11
  171.2 40.2 all-gather.19
  213.5 40.1 all-gather.17
  256.4 135.4 reduce-scatter.1
where the time goes:
time: 402 us; the launch traced here: 399 us
  waiting for transfers between devices  211 us (52%)
  other arithmetic  104 us (26%)
  blocking collectives  36.1 us (9%)
  between operations  17.7 us (4%)
  matrix products  13.7 us (3%)
  local copies, waits for them, and re-layouts  11.1 us (3%)
  starting transfers between devices  4.37 us (1%)
    reduce_scatter x1, waiting for transfers between devices, local(): lax.psum_scatter(lax.dot_general(normed_out, grad_local, (((0,), (0,)), (...  111 us
    all_gather x4, waiting for transfers between devices, carried_in(): pieces = jax.tree.map(lambda part: lax.all_gather(part, axis), value)  70.9 us
    convert_element_type x60, other arithmetic, carry_combine(): following[0].astype(jnp.float32)[:, None, None]  47.6 us
    select_n x60, other arithmetic, step(): jnp.where(position < mine, new, old)  44.8 us
    unnamed x1, blocking collectives  36.1 us
    all_gather x1, waiting for transfers between devices, local(): full_weight = lax.all_gather(out_weight, ('dp', 'ctx'), axis=0, tiled=True)  28.4 us
  transfers between devices with their start and end apart: 8, of which 5 were waited for; matrix products, arithmetic and copies ran while one was open for 30% of the time, Pallas kernels for 0%

commit v1 on v0

v1 whole, which is shorter than its diff:
```python
import functools

import jax
import jax.numpy as jnp
from jax import lax
from jax.experimental import pallas as pl
from jax.experimental.pallas import tpu as pltpu
from jax.sharding import PartitionSpec as P

eps = 1e-05
MESH = pl.DeviceIdType.MESH
f32 = jnp.float32
bf16 = jnp.bfloat16
AUX = 16


def matmul(a, b, ca, cb, precision=None):
    return lax.dot_general(
        a, b, (((ca,), (cb,)), ((), ())), preferred_element_type=f32, precision=precision
    )


def kernel(
    dp,
    n,
    fused,
    feat,
    gate,
    state_in,
    state_out,
    step,
    rate,
    users,
    norm_gain,
    weight,
    out_grad,
    mixed,
    feature_grad,
    weight_grad,
    scratch,
):
    me = lax.axis_index("ctx")
    x = lax.axis_index("dp")
    tokens, inner_dim = feat.shape
    heads = step.shape[0]
    width = inner_dim // heads
    nstate = state_in.shape[1]
    share = 2 * heads * nstate // n
    half = n // 2

    barrier = pltpu.get_barrier_semaphore()

    def greet(k, _):
        pl.semaphore_signal(
            barrier, inc=1, device_id={"ctx": lax.rem(me + k, n)}, device_id_type=MESH
        )
        return 0

    lax.fori_loop(1, n, greet, 0)
    if fused:
        pl.semaphore_signal(barrier, inc=1, device_id={"dp": 1 - x}, device_id_type=MESH)
    pl.semaphore_wait(barrier, n - 1 + (1 if fused else 0))

    if fused:
        count_a = n // 4
        a, b, c = me // 4, (me // 2) % 2, me % 2
        y_peer = {"ctx": a * 4 + (1 - b) * 2 + c}
        x_peer = {"dp": 1 - x}
        core_peer = {"ctx": a * 4 + b * 2 + (1 - c)}
        full, wss, wrs = scratch["full"], scratch["wss"], scratch["wrs"]
        full[x, a, b, c] = weight[...]

        def z_copy(source, slot, to):
            return pltpu.make_async_remote_copy(
                src_ref=weight,
                dst_ref=full.at[x, source, b, c],
                send_sem=wss.at[slot],
                recv_sem=wrs.at[source],
                device_id={"ctx": to * 4 + b * 2 + c},
                device_id_type=MESH,
            )

        def w_copy(view, slot, peer):
            return pltpu.make_async_remote_copy(
                src_ref=view,
                dst_ref=view,
                send_sem=wss.at[count_a + slot],
                recv_sem=wrs.at[count_a + slot],
                device_id=peer,
                device_id_type=MESH,
            )

        for k in range(1, count_a):
            z_copy(a, k, lax.rem(a + k, count_a)).start()
        sent_y = w_copy(full.at[x, :, b, c], 0, y_peer)
        got_y = w_copy(full.at[x, :, 1 - b, c], 0, y_peer)
        sent_x = w_copy(full.at[x, :, :, c], 1, x_peer)
        got_x = w_copy(full.at[1 - x, :, :, c], 1, x_peer)
        sent_core = w_copy(full.at[:, :, :, c], 2, core_peer)
        got_core = w_copy(full.at[:, :, :, 1 - c], 2, core_peer)

    row_of = lax.broadcasted_iota(jnp.int32, (tokens, tokens), 0)
    column_of = lax.broadcasted_iota(jnp.int32, (tokens, tokens), 1)
    head_of = lax.broadcasted_iota(jnp.int32, (heads, 1), 0)
    rates = jnp.zeros((heads, 1), f32)
    for h in range(heads):
        rates = jnp.where(head_of == h, rate[h], rates)
    logdec = -step[...] * rates
    upto = (row_of <= column_of).astype(f32)
    cumulative = matmul(logdec, upto, 1, 0, lax.Precision.HIGHEST)
    user_row = users[...].astype(f32)
    stacked = jnp.concatenate(
        [
            cumulative,
            jnp.broadcast_to(user_row, (8, tokens)),
            jnp.zeros((tokens - heads - 8, tokens), f32),
        ],
        axis=0,
    )
    turned = stacked.T
    along = turned[:, :heads]
    user_col = turned[:, heads : heads + 1]
    total = along[tokens - 1 : tokens, :]
    first_user = user_col[0:1, :]
    last_user = user_col[tokens - 1 : tokens, :]
    to_end = jnp.exp(total - along)
    from_start = jnp.exp(along)
    fwd_scale = jnp.where(user_col == last_user, to_end, 0.0)
    rev_scale = jnp.where(user_col == first_user, from_start, 0.0)
    passing = jnp.exp(total)
    aux_row = lax.broadcasted_iota(jnp.int32, (AUX, width), 0)

    def send_states(which, values, keys):
        st, ra = scratch["st"].at[which], scratch["ra"].at[which]
        keys_wide = keys[...].astype(f32)
        for h in range(heads):
            v = values[:, h * width : (h + 1) * width]
            both = jnp.concatenate(
                [
                    (keys_wide * fwd_scale[:, h : h + 1]).astype(bf16),
                    (keys_wide * rev_scale[:, h : h + 1]).astype(bf16),
                ],
                axis=1,
            )
            states = matmul(both, v, 0, 0).astype(bf16)
            for d in range(2):
                aux = jnp.where(
                    aux_row == 0, passing[:, h : h + 1], last_user if d == 0 else first_user
                ).astype(bf16)
                for q in range(nstate // share):
                    unit = (d * heads + h) * (nstate // share) + q
                    start = d * nstate + q * share
                    st[unit, 0:share, :] = states[start : start + share]
                    st[unit, share : share + AUX, :] = aux

        def send(k, _):
            to = lax.rem(me + k, n)
            pltpu.make_async_remote_copy(
                src_ref=st.at[to],
                dst_ref=ra.at[me],
                send_sem=scratch["a_send"].at[which, to],
                recv_sem=scratch["a_recv"].at[which, me],
                device_id={"ctx": to},
                device_id_type=MESH,
            ).start()
            return 0

        lax.fori_loop(1, n, send, 0)
        ra[me] = st[me]

    def arrival(name, which, ref_from, ref_to, j):
        return pltpu.make_async_remote_copy(
            src_ref=ref_from.at[j],
            dst_ref=ref_to.at[j],
            send_sem=scratch[name + "_send"].at[which, j],
            recv_sem=scratch[name + "_recv"].at[which, j],
            device_id={"ctx": j},
            device_id_type=MESH,
        )

    def scan_states(which):
        st, ra = scratch["st"].at[which], scratch["ra"].at[which]
        sb, rb = scratch["sb"].at[which], scratch["rb"].at[which]
        backward = me // half

        def body(p, carry):
            running, previous = carry
            j = p + backward * (n - 1 - 2 * p)

            @pl.when(j != me)
            def _():
                arrival("a", which, st, ra, j).wait_recv()

            sb[j, 0:share, :] = running.astype(bf16)
            sb[j, share : share + AUX, :] = jnp.broadcast_to(previous, (AUX, width)).astype(bf16)

            @pl.when(j != me)
            def _():
                pltpu.make_async_remote_copy(
                    src_ref=sb.at[j],
                    dst_ref=rb.at[me],
                    send_sem=scratch["b_send"].at[which, j],
                    recv_sem=scratch["b_recv"].at[which, me],
                    device_id={"ctx": j},
                    device_id_type=MESH,
                ).start()

            block = ra[j].astype(f32)
            boundary = block[share + 1 : share + 2]
            gain = jnp.where(boundary == previous, block[share : share + 1], 0.0)
            running = (gain * running + block[0:share]).astype(bf16).astype(f32)
            return running, boundary

        lax.fori_loop(
            0, n, body, (jnp.zeros((share, width), f32), jnp.full((1, width), -1.0, f32))
        )
        rb[me] = sb[me]

    def wait_carries(which):
        sb, rb = scratch["sb"].at[which], scratch["rb"].at[which]

        def body(k, _):
            arrival("b", which, sb, rb, lax.rem(me + k, n)).wait_recv()
            return 0

        lax.fori_loop(1, n, body, 0)

    def finish_sends(which):
        st, ra = scratch["st"].at[which], scratch["ra"].at[which]
        sb, rb = scratch["sb"].at[which], scratch["rb"].at[which]

        def body(k, _):
            j = lax.rem(me + k, n)
            arrival("a", which, st, ra, j).wait_send()
            arrival("b", which, sb, rb, j).wait_send()
            return 0

        lax.fori_loop(1, n, body, 0)

    def apply_carries(which, reads, h):
        rb = scratch["rb"].at[which]
        pieces = nstate // share
        before_user = rb[0, share : share + 1, 0:1].astype(f32)
        after_user = rb[n - 1, share : share + 1, 0:1].astype(f32)
        early = jnp.where(user_col == before_user, from_start[:, h : h + 1], 0.0)
        late = jnp.where(user_col == after_user, to_end[:, h : h + 1], 0.0)
        parts = []
        for d in range(2):
            base = (d * heads + h) * pieces
            if pieces == 1:
                state = rb[base, 0:share, :]
            else:
                state = jnp.concatenate([rb[base + q, 0:share, :] for q in range(pieces)], axis=0)
            parts.append(matmul(reads[...], state, 1, 0))
        return early * parts[0] + late * parts[1]

    send_states(0, feat, state_in)
    if fused:
        for k in range(1, count_a):
            source = lax.rem(a + k, count_a)
            z_copy(source, k, a).wait_recv()
        sent_y.start()

    scores = matmul(state_out[...], state_in[...], 1, 1)
    scores = jnp.where(row_of == column_of, 2.0 * scores, scores)
    scores = jnp.where(user_col == user_row, scores, 0.0)
    mixw, y = scratch["mixw"], scratch["y"]
    for h in range(heads):
        spread = jnp.abs(along[:, h : h + 1] - cumulative[h : h + 1, :])
        weights = (scores * jnp.exp(-spread)).astype(bf16)
        mixw[h] = weights
        cols = slice(h * width, (h + 1) * width)
        y[:, cols] = matmul(weights, feat[:, cols], 1, 0)
    if fused:
        got_y.wait_recv()
        sent_x.start()
    silu, cot, normed, grad_mixed = (
        scratch["silu"],
        scratch["cot"],
        scratch["normed"],
        scratch["grad_mixed"],
    )
    gates = gate[...].astype(f32)
    silu[...] = gates / (1.0 + jnp.exp(-gates))
    scan_states(0)
    if fused:
        got_x.wait_recv()
        sent_core.start()
        got_core.wait_recv()
        whole = full[...].reshape(inner_dim, weight.shape[1])
    else:
        whole = weight[...]
    scale = norm_gain[...].astype(f32)
    cot[...] = matmul(out_grad[...], whole, 1, 1) * scale
    wait_carries(0)
    for h in range(heads):
        cols = slice(h * width, (h + 1) * width)
        y[:, cols] = (y[:, cols] + apply_carries(0, state_out, h)) * silu[:, cols]
    gated = y[...]
    multiplier = lax.rsqrt(jnp.mean(gated * gated, axis=1, keepdims=True) + eps)
    back = cot[...]
    slope = jnp.mean(back * gated, axis=1, keepdims=True) * multiplier * multiplier
    grad_mixed[...] = ((back - gated * slope) * multiplier * silu[...]).astype(bf16)
    send_states(1, grad_mixed, state_out)

    normed[...] = (y[...] * multiplier * scale).astype(bf16)
    if fused:
        part = scratch["part"]
        rss, rrs = scratch["rss"], scratch["rrs"]
        rows = weight.shape[0]
        part[...] = matmul(normed[...], out_grad[...], 0, 0).astype(bf16).reshape(part.shape)

        def r_copy(source, target, slot, peer):
            return pltpu.make_async_remote_copy(
                src_ref=source,
                dst_ref=target,
                send_sem=rss.at[slot],
                recv_sem=rrs.at[slot],
                device_id=peer,
                device_id_type=MESH,
            )

        one, two, three, four = (scratch[name] for name in ("one", "two", "three", "four"))
        r_core = r_copy(part.at[:, :, :, 1 - c], one, count_a, core_peer)
        r_x = r_copy(one.at[1 - x], two, count_a + 1, x_peer)
        r_y = r_copy(two.at[:, 1 - b], three, count_a + 2, y_peer)
        r_core.start()
    else:
        weight_grad[...] = matmul(normed[...], out_grad[...], 0, 0)

    for h in range(heads):
        cols = slice(h * width, (h + 1) * width)
        y[:, cols] = matmul(mixw[h], grad_mixed[:, cols], 0, 0)
    if fused:
        r_core.wait_recv()
        one[...] = (one[...].astype(f32) + part[:, :, :, c].astype(f32)).astype(bf16)
        r_x.start()
    scan_states(1)
    mixed[...] = matmul(normed[...], whole, 1, 0).astype(bf16)
    if fused:
        r_x.wait_recv()
        two[...] = (two[...].astype(f32) + one[x].astype(f32)).astype(bf16)
        r_y.start()
    wait_carries(1)
    for h in range(heads):
        cols = slice(h * width, (h + 1) * width)
        feature_grad[:, cols] = (y[:, cols] + apply_carries(1, state_in, h)).astype(bf16)
    if fused:
        r_y.wait_recv()
        three[...] = (three[...].astype(f32) + two[:, b].astype(f32)).astype(bf16)

        def last_copy(k, source, target, to):
            return pltpu.make_async_remote_copy(
                src_ref=three.at[source],
                dst_ref=four.at[target],
                send_sem=rss.at[k],
                recv_sem=rrs.at[target],
                device_id={"ctx": to * 4 + b * 2 + c},
                device_id_type=MESH,
            )

        for k in range(1, count_a):
            to = lax.rem(a + k, count_a)
            last_copy(k, to, a, to).start()
        result = three[a].astype(f32)
        for k in range(1, count_a):
            source = lax.rem(a + k, count_a)
            last_copy(k, source, source, source).wait_recv()
            result = result + four[source].astype(f32)
        weight_grad[...] = result
        for k in range(1, count_a):
            to = lax.rem(a + k, count_a)
            last_copy(k, to, a, to).wait_send()
            z_copy(a, k, to).wait_send()
        for copy in (sent_y, sent_x, sent_core, r_core, r_x, r_y):
            copy.wait_send()
    finish_sends(0)
    finish_sends(1)


def local(
    dp,
    n,
    features,
    gate_in,
    state_in,
    state_out,
    step_size,
    decay_rate,
    user_ids,
    norm_gain,
    out_weight,
    out_grad,
):
    tokens, inner_dim = features.shape[1:]
    heads = step_size.shape[1]
    width = inner_dim // heads
    nstate = state_in.shape[2]
    rows, out_dim = out_weight.shape
    fused = dp == 2 and n == 16 and rows % 16 == 0
    share = 2 * heads * nstate // n
    states = pltpu.VMEM((2, n, share + AUX, width), bf16)
    dma = pltpu.SemaphoreType.DMA
    scratch = dict(
        st=states,
        ra=states,
        sb=states,
        rb=states,
        a_send=dma((2, n)),
        a_recv=dma((2, n)),
        b_send=dma((2, n)),
        b_recv=dma((2, n)),
        mixw=pltpu.VMEM((heads, tokens, tokens), bf16),
        y=pltpu.VMEM((tokens, inner_dim), f32),
        silu=pltpu.VMEM((tokens, inner_dim), f32),
        cot=pltpu.VMEM((tokens, inner_dim), f32),
        normed=pltpu.VMEM((tokens, inner_dim), bf16),
        grad_mixed=pltpu.VMEM((tokens, inner_dim), bf16),
    )
    if fused:
        count_a = n // 4
        sems = dma((count_a + 3,))
        scratch.update(
            full=pltpu.VMEM((2, count_a, 2, 2, rows, out_dim), bf16),
            part=pltpu.VMEM((2, count_a, 2, 2, rows, out_dim), bf16),
            one=pltpu.VMEM((2, count_a, 2, rows, out_dim), bf16),
            two=pltpu.VMEM((count_a, 2, rows, out_dim), bf16),
            three=pltpu.VMEM((count_a, rows, out_dim), bf16),
            four=pltpu.VMEM((count_a, rows, out_dim), bf16),
            wss=sems,
            wrs=sems,
            rss=sems,
            rrs=sems,
        )
        held = out_weight
    else:
        held = lax.all_gather(out_weight, ("dp", "ctx"), axis=0, tiled=True)
    names = list(scratch)

    def body(*refs):
        kernel(dp, n, fused, *refs[:13], dict(zip(names, refs[13:])))

    vmem = pl.BlockSpec(memory_space=pltpu.VMEM)
    mixed, feature_grad, weight_grad = pl.pallas_call(
        body,
        out_shape=(
            jax.ShapeDtypeStruct((tokens, out_dim), bf16),
            jax.ShapeDtypeStruct((tokens, inner_dim), bf16),
            jax.ShapeDtypeStruct(held.shape, f32),
        ),
        in_specs=[vmem] * 5 + [pl.BlockSpec(memory_space=pltpu.SMEM)] + [vmem] * 4,
        out_specs=(vmem, vmem, vmem),
        scratch_shapes=list(scratch.values()),
        compiler_params=pltpu.CompilerParams(
            collective_id=0, has_side_effects=True, vmem_limit_bytes=40 << 20
        ),
        name="mixer",
    )(
        features[0],
        gate_in[0],
        state_in[0],
        state_out[0],
        step_size[0],
        decay_rate,
        user_ids,
        norm_gain.reshape(1, -1),
        held,
        out_grad[0],
    )
    if not fused:
        weight_grad = lax.psum_scatter(
            weight_grad, ("dp", "ctx"), scatter_dimension=0, tiled=True
        )
    return mixed[None], feature_grad[None], weight_grad


def solution(mesh):
    placed = (
        P("dp", "ctx", None),
        P("dp", "ctx", None),
        P("dp", "ctx", None),
        P("dp", "ctx", None),
        P("dp", None, "ctx"),
        P(),
        P("dp", "ctx"),
        P(),
        P(("dp", "ctx"), None),
        P("dp", "ctx", None),
    )
    return jax.shard_map(
        functools.partial(local, mesh.shape["dp"], mesh.shape["ctx"]),
        mesh=mesh,
        in_specs=placed,
        out_specs=(P("dp", "ctx", None), P("dp", "ctx", None), P(("dp", "ctx"), None)),
        check_vma=False,
    )
```

time: 402 us -> 63.5 us (0.16)
  waiting for transfers between devices: 211 us -> 0 us
  other arithmetic: 104 us -> 0 us
  Pallas kernels: 0 us -> 55.4 us
  blocking collectives: 36.1 us -> 0 us
  between operations: 17.7 us -> 0.7 us
  matrix products: 13.7 us -> 0 us
  starting transfers between devices: 4.37 us -> 0 us
    reduce_scatter x1 -> x0, waiting for transfers between devices: 111 us -> none  [local(): lax.psum_scatter(lax.dot_general(normed_out, grad_local, (((0,), (0,)), (...]
    all_gather x5 -> x0, waiting for transfers between devices: 99.3 us -> none  [the longest x4 70.9 us: carried_in(): pieces = jax.tree.map(lambda part: lax.all_gather(part, axis), value)]
    pallas_call x0 -> x1, Pallas kernels: none -> 55.4 us  [local(): pl.pallas_call(body, out_shape=(jax.ShapeDtypeStruct((tokens, out_dim), b...]
    convert_element_type x64 -> x0, other arithmetic: 50 us -> none  [the longest x60 47.6 us: carry_combine(): following[0].astype(jnp.float32)[:, None, None]]
    select_n x60 -> x0, other arithmetic: 44.8 us -> none  [step(): jnp.where(position < mine, new, old)]
    unnamed x1 -> x0, blocking collectives: 36.1 us -> none
    dot_general x15 -> x0, matrix products: 13.7 us -> none  [the longest x2 2.36 us: block_terms(): jnp.dot(reads, keys_in.T, preferred_element_type=jnp.float32)]
    mul x4 -> x0, other arithmetic: 5.22 us -> none  [the longest x2 3.86 us: apply_carries(): jnp.exp(cumulative) * (user_row == before_user).astype(jnp.float32)[None]]
  transfers between devices with their start and end apart: 8 -> 0, of which waited for: 5 -> 0; matrix products, arithmetic and copies ran while one was open for 30% -> 0% of each run, Pallas kernels for 0% -> 0%
where the time goes in v1:
time: 63.5 us; the launch traced here: 63.2 us
  Pallas kernels  55.4 us (87%)
  local copies, waits for them, and re-layouts  7.1 us (11%)
  between operations  0.7 us (1%)
    pallas_call x1, Pallas kernels, local(): pl.pallas_call(body, out_shape=(jax.ShapeDtypeStruct((tokens, out_dim), b...  55.4 us
    unnamed x23, local copies, waits for them, and re-layouts  7.1 us

profile of v1, /device:TPU:0, one launch (start us, length us, event | category | flops | bytes accessed | tf_op | source)
XLA Modules:
  0.0 63.2 jit_solution(7534991977242619055)
XLA Ops:
  0.6 0.0 copy-start.8
  0.6 0.7 %copy-done.8 = bf16[1024]{0:T(1024)(128)(2,1)S(1)} copy-done((bf16[1024]{0:T(1024)(128)(2,1)S(1)}, bf16[1024]{0:T(1024)(128)(2,1)}, u32[]{:S(2)}) %copy-start.8) | copy-done | bytes 2072
  1.3 0.0 copy-start.7
  1.3 0.8 %copy.13 = bf16[1,128,64]{2,1,0:T(8,128)(2,1)S(1)} copy(bf16[1,128,64]{1,2,0:T(8,128)(2,1)} %param.12) | data formatting | bytes 32768 | tf_op args[2]
  2.2 0.0 copy-start.3
  2.2 0.0 copy-done.7
  2.2 0.0 copy-start.4
  2.2 0.1 copy.14
  2.3 0.0 copy-start.5
  2.3 0.0 copy-start.6
  2.3 0.6 copy-done.3
  2.9 0.0 copy-done.4
  2.9 0.0 copy-done.5
  3.0 0.0 copy-done.6
  3.0 0.0 copy-start
  3.0 0.9 %copy-done = bf16[1,128,1024]{2,1,0:T(8,128)(2,1)S(1)} copy-done((bf16[1,128,1024]{2,1,0:T(8,128)(2,1)S(1)}, bf16[1,128,1024]{2,1,0:T(8,128)(2,1)}, u32[]{:S(2)}) %copy-start) | copy-done | bytes 262168
  3.9 0.0 copy-start.1
  3.9 0.9 %copy-done.1 = bf16[1,128,1024]{2,1,0:T(8,128)(2,1)S(1)} copy-done((bf16[1,128,1024]{2,1,0:T(8,128)(2,1)S(1)}, bf16[1,128,1024]{2,1,0:T(8,128)(2,1)}, u32[]{:S(2)}) %copy-start.1) | copy-done | bytes 262168
  4.9 0.0 copy-start.2
  4.9 0.9 %copy-done.2 = bf16[1,128,512]{2,1,0:T(8,128)(2,1)S(1)} copy-done((bf16[1,128,512]{2,1,0:T(8,128)(2,1)S(1)}, bf16[1,128,512]{2,1,0:T(8,128)(2,1)}, u32[]{:S(2)}) %copy-start.2) | copy-done | bytes 131096
  5.8 55.4 %mixer.1 = (bf16[128,512]{1,0:T(8,128)(2,1)S(1)}, bf16[128,1024]{1,0:T(8,128)(2,1)S(1)}, f32[32,512]{1,0:T(8,128)S(1)}) custom-call(bf16[128,1024]{1,0:T(8,128)(2,1)S(1)} %bitcast.8, bf16[128,1024]{1,0:T(8,128)(2,1)S(1)} %bitcast.9, bf16[128,64]{1,0:T(8,128)(2,1)S(1)} %bitcast.11, bf16[128,64]{1,0:T(8,128)(2,1)S(1)} %bitcast.12, f32[8,128]{1,0:T(8,128)S(1)} %bitcast.15, ...), custom_call_target="tpu_custom_call" | custom-call | tf_op jit(solution)/shard_map/mixer/pallas_call | solution.py:444
  61.2 0.7 %copy.18 = bf16[1,128,512]{2,1,0:T(8,128)(2,1)} copy(bf16[1,128,512]{2,1,0:T(8,128)(2,1)S(1)} %bitcast.13) | data formatting | bytes 262144
  61.8 0.7 %copy.19 = bf16[1,128,1024]{2,1,0:T(8,128)(2,1)} copy(bf16[1,128,1024]{2,1,0:T(8,128)(2,1)S(1)} %bitcast.10) | data formatting | bytes 524288
  62.5 0.6 copy.20
  (1 shorter events, 0.0 us)
Async XLA Ops:
  0.6 0.7 %copy-start.8 = (bf16[1024]{0:T(1024)(128)(2,1)S(1)}, bf16[1024]{0:T(1024)(128)(2,1)}, u32[]{:S(2)}) copy-start(bf16[1024]{0:T(1024)(128)(2,1)} %param.17) | copy-start | bytes 6148
  1.3 0.9 %copy-start.7 = (bf16[1,128,64]{1,2,0:T(8,128)(2,1)S(1)}, bf16[1,128,64]{1,2,0:T(8,128)(2,1)}, u32[]{:S(2)}) copy-start(bf16[1,128,64]{1,2,0:T(8,128)(2,1)} %param.13) | copy-start | bytes 49156
  2.2 0.8 %copy-start.3 = (bf16[32,512]{1,0:T(8,128)(2,1)S(1)}, bf16[32,512]{1,0:T(8,128)(2,1)}, u32[]{:S(2)}) copy-start(bf16[32,512]{1,0:T(8,128)(2,1)} %refs_8_.1) | copy-start | bytes 98308
  2.2 0.8 %copy-start.4 = (f32[1,8,128]{2,1,0:T(8,128)S(1)}, f32[1,8,128]{2,1,0:T(8,128)}, u32[]{:S(2)}) copy-start(f32[1,8,128]{2,1,0:T(8,128)} %param.14) | copy-start | bytes 12292
  2.3 0.7 %copy-start.5 = (f32[8]{0:T(128)S(1)}, f32[8]{0:T(128)}, u32[]{:S(2)}) copy-start(f32[8]{0:T(128)} %refs_5_.1) | copy-start | bytes 100
  2.3 0.7 %copy-start.6 = (s32[1,128]{1,0:T(1,128)S(1)}, s32[1,128]{1,0:T(1,128)}, u32[]{:S(2)}) copy-start(s32[1,128]{1,0:T(1,128)} %refs_6_.1) | copy-start | bytes 1540
  3.0 0.9 %copy-start = (bf16[1,128,1024]{2,1,0:T(8,128)(2,1)S(1)}, bf16[1,128,1024]{2,1,0:T(8,128)(2,1)}, u32[]{:S(2)}) copy-start(bf16[1,128,1024]{2,1,0:T(8,128)(2,1)} %param.10) | copy-start | bytes 786436
  3.9 0.9 %copy-start.1 = (bf16[1,128,1024]{2,1,0:T(8,128)(2,1)S(1)}, bf16[1,128,1024]{2,1,0:T(8,128)(2,1)}, u32[]{:S(2)}) copy-start(bf16[1,128,1024]{2,1,0:T(8,128)(2,1)} %param.11) | copy-start | bytes 786436
  4.9 0.9 %copy-start.2 = (bf16[1,128,512]{2,1,0:T(8,128)(2,1)S(1)}, bf16[1,128,512]{2,1,0:T(8,128)(2,1)}, u32[]{:S(2)}) copy-start(bf16[1,128,512]{2,1,0:T(8,128)(2,1)} %param.19) | copy-start | bytes 393220

commit v2 on v1

v2 whole, which is shorter than its diff:
```python
import functools

import jax
import jax.numpy as jnp
from jax import lax
from jax.experimental import pallas as pl
from jax.experimental.pallas import tpu as pltpu
from jax.sharding import PartitionSpec as P

eps = 1e-05
MESH = pl.DeviceIdType.MESH
f32 = jnp.float32
bf16 = jnp.bfloat16
AUX = 16


def matmul(a, b, ca, cb, precision=None):
    return lax.dot_general(
        a, b, (((ca,), (cb,)), ((), ())), preferred_element_type=f32, precision=precision
    )


def kernel(
    n,
    fused,
    feat_hbm,
    gate_hbm,
    keys_t,
    reads_t,
    step,
    rate,
    users,
    norm_gain,
    weight_hbm,
    out_grad_hbm,
    mixed,
    feature_grad,
    weight_grad,
    scratch,
):
    me = lax.axis_index("ctx")
    x = lax.axis_index("dp")
    chips = n // 2
    chip, c = me // 2, me % 2
    feat, gate, out_grad = scratch["feat"], scratch["gate"], scratch["out_grad"]
    tokens, inner_dim = feat.shape
    heads = step.shape[0]
    width = inner_dim // heads
    nstate = keys_t.shape[0]
    share = 2 * heads * nstate // n
    pieces = nstate // share
    core_peer = {"ctx": chip * 2 + 1 - c}
    loads = scratch["loads"]

    def signal(to):
        pl.semaphore_signal(barrier, inc=1, device_id=to, device_id_type=MESH)

    def remote(source, target, send_sem, recv_sem, to):
        return pltpu.make_async_remote_copy(
            src_ref=source,
            dst_ref=target,
            send_sem=send_sem,
            recv_sem=recv_sem,
            device_id=to,
            device_id_type=MESH,
        )

    get_feat = pltpu.make_async_copy(feat_hbm, feat, loads.at[0])
    get_gate = pltpu.make_async_copy(gate_hbm, gate, loads.at[1])
    get_grad = pltpu.make_async_copy(out_grad_hbm, out_grad, loads.at[2])
    if fused:
        count_a = n // 4
        a, b = me // 4, (me // 2) % 2
        full, wss, wrs = scratch["full"], scratch["wss"], scratch["wrs"]
        rows, out_dim = weight_hbm.shape
        get_weight = pltpu.make_async_copy(weight_hbm, full.at[x, a, b, c], loads.at[3])
    else:
        get_weight = pltpu.make_async_copy(weight_hbm, scratch["full"], loads.at[3])
    get_weight.start()
    get_feat.start()
    get_grad.start()
    get_gate.start()

    barrier = pltpu.get_barrier_semaphore()

    def greet(k, _):
        signal({"ctx": lax.rem(chip + k, chips) * 2 + c})
        return 0

    lax.fori_loop(1, chips, greet, 0)
    signal(core_peer)
    if fused:
        signal({"dp": 1 - x})
    pl.semaphore_wait(barrier, chips + (1 if fused else 0))

    if fused:
        get_weight.wait()
        fx = x + c * (1 - 2 * x)
        fb = b + (1 - c) * (1 - 2 * b)
        y_peer = {"dp": x, "ctx": a * 4 + (1 - b) * 2 + c}
        x_peer = {"dp": 1 - x, "ctx": me}
        first_peer = {
            "dp": 1 - fx,
            "ctx": a * 4 + (1 - fb) * 2 + c,
        }
        second_peer = {"dp": fx, "ctx": a * 4 + fb * 2 + c}

        def z_copy(source, slot, to):
            view = full.at[x, source, b, c]
            return remote(
                view, view, wss.at[slot], wrs.at[source], {"ctx": to * 4 + b * 2 + c}
            )

        def w_copy(view, slot, peer):
            return remote(view, view, wss.at[count_a + slot], wrs.at[count_a + slot], peer)

        for k in range(1, count_a):
            z_copy(a, k, lax.rem(a + k, count_a)).start()
        w_y = w_copy(full.at[x, :, b, c], 0, y_peer)
        w_x = w_copy(full.at[x, :, b, c], 1, x_peer)
        w_on = w_copy(full.at[fx, :, fb, c], 2, first_peer)
        w_core = w_copy(full.at[:, :, :, c], 3, core_peer)

    row_of = lax.broadcasted_iota(jnp.int32, (tokens, tokens), 0)
    column_of = lax.broadcasted_iota(jnp.int32, (tokens, tokens), 1)
    head_of = lax.broadcasted_iota(jnp.int32, (heads, 1), 0)
    rates = jnp.zeros((heads, 1), f32)
    for h in range(heads):
        rates = jnp.where(head_of == h, rate[h], rates)
    logdec = -step[...] * rates
    upto = (row_of <= column_of).astype(f32)
    cumulative = matmul(logdec, upto, 1, 0, lax.Precision.HIGHEST)
    total = cumulative[:, tokens - 1 : tokens]
    user_row = users[...].astype(f32)
    first_user = user_row[:, 0:1]
    last_user = user_row[:, tokens - 1 : tokens]
    from_start = jnp.exp(cumulative)
    to_end = jnp.exp(total - cumulative)
    passing = jnp.exp(total)
    fwd_scale = jnp.where(user_row == last_user, to_end, 0.0)
    rev_scale = jnp.where(user_row == first_user, from_start, 0.0)
    stacked = jnp.concatenate(
        [
            cumulative,
            from_start,
            to_end,
            jnp.broadcast_to(user_row, (8, tokens)),
            jnp.zeros((tokens - 3 * heads - 8, tokens), f32),
        ],
        axis=0,
    ).T
    along = stacked[:, 0:heads]
    start_col = stacked[:, heads : 2 * heads]
    end_col = stacked[:, 2 * heads : 3 * heads]
    user_col = stacked[:, 3 * heads : 3 * heads + 1]
    own_col = jnp.where(c == 1, start_col, end_col)
    other_col = jnp.where(c == 1, end_col, start_col)
    aux_row = lax.broadcasted_iota(jnp.int32, (AUX, width), 0)

    def chip_copy(name, which, source, target, index, slot, to):
        return remote(
            source.at[index],
            target.at[slot],
            scratch[name + "_send"].at[which, to],
            scratch[name + "_recv"].at[which, slot],
            {"ctx": to * 2 + c},
        )

    def refs(which):
        return [scratch[name].at[which] for name in ("st", "pt", "ct", "ra", "sb", "rb", "rx")]

    def pair_copy(which):
        st, pt = refs(which)[:2]
        return remote(
            st.at[c], pt, scratch["p_send"].at[which], scratch["p_recv"].at[which], core_peer
        )

    def relay_copy(which, u):
        rb, rx = refs(which)[5:]
        return remote(
            rb.at[u],
            rx.at[u],
            scratch["x_send"].at[which, u],
            scratch["x_recv"].at[which, u],
            core_peer,
        )

    def make_states(which, values, keys):
        st = refs(which)[0]
        wide = keys[...].astype(f32)
        for h in range(heads):
            v = values[:, h * width : (h + 1) * width]
            both = jnp.concatenate(
                [wide * fwd_scale[h : h + 1, :], wide * rev_scale[h : h + 1, :]], axis=0
            ).astype(bf16)
            states = matmul(both, v, 1, 0).astype(bf16)
            for d in range(2):
                aux = jnp.where(
                    aux_row == 0, passing[h : h + 1, :], last_user if d == 0 else first_user
                ).astype(bf16)
                for q in range(pieces):
                    start = d * nstate + q * share
                    st[d, h * pieces + q, 0:share, :] = states[start : start + share]
                    st[d, h * pieces + q, share : share + AUX, :] = aux
        pair_copy(which).start()

    def send_chip(which):
        st, pt, ct, ra, sb, rb, rx = refs(which)
        pair_copy(which).wait_recv()
        mine, theirs = st[1 - c].astype(f32), pt[...].astype(f32)
        gain = mine[:, share : share + 1]
        same = mine[:, share + 1 : share + 2] == theirs[:, share + 1 : share + 2]
        ct[:, 0:share, :] = (
            jnp.where(same, gain, 0.0) * theirs[:, 0:share] + mine[:, 0:share]
        ).astype(bf16)
        ct[:, share : share + AUX, :] = jnp.where(
            aux_row[None] == 0, mine[:, share:] * theirs[:, share:], mine[:, share:]
        ).astype(bf16)

        def send(k, _):
            to = lax.rem(chip + k, chips)
            chip_copy("a", which, ct, ra, to, chip, to).start()
            return 0

        lax.fori_loop(1, chips, send, 0)
        ra[chip] = ct[chip]

    def scan_states(which):
        st, pt, ct, ra, sb, rb, rx = refs(which)

        def body(p, carry):
            running, previous = carry
            j = p + (1 - c) * (chips - 1 - 2 * p)

            @pl.when(j != chip)
            def _():
                chip_copy("a", which, ct, ra, j, j, j).wait_recv()

            sb[j, 0:share, :] = running.astype(bf16)
            sb[j, share : share + AUX, :] = jnp.broadcast_to(previous, (AUX, width)).astype(bf16)

            @pl.when(j != chip)
            def _():
                chip_copy("b", which, sb, rb, j, chip, j).start()

            block = ra[j].astype(f32)
            boundary = block[share + 1 : share + 2]
            gain = jnp.where(boundary == previous, block[share : share + 1], 0.0)
            running = (gain * running + block[0:share]).astype(bf16).astype(f32)
            return running, boundary

        lax.fori_loop(
            0, chips, body, (jnp.zeros((share, width), f32), jnp.full((1, width), -1.0, f32))
        )
        rb[chip] = sb[chip]
        relay_copy(which, chip).start()

    def relay(which):
        st, pt, ct, ra, sb, rb, rx = refs(which)

        def body(k, _):
            u = lax.rem(chip + k, chips)
            chip_copy("b", which, sb, rb, u, u, u).wait_recv()
            relay_copy(which, u).start()
            return 0

        lax.fori_loop(1, chips, body, 0)
        theirs, past = pt[...].astype(f32), rb[...].astype(f32)
        same = theirs[:, share + 1 : share + 2] == past[:, share + 1 : share + 2]
        scratch["oc"][...] = (
            jnp.where(same, theirs[:, share : share + 1], 0.0) * past[:, 0:share]
            + theirs[:, 0:share]
        ).astype(bf16)

        def arrive(u, _):
            relay_copy(which, u).wait_recv()
            return 0

        lax.fori_loop(0, chips, arrive, 0)

    def finish_sends(which):
        st, pt, ct, ra, sb, rb, rx = refs(which)
        pair_copy(which).wait_send()
        relay_copy(which, chip).wait_send()

        def body(k, _):
            j = lax.rem(chip + k, chips)
            chip_copy("a", which, ct, ra, j, j, j).wait_send()
            chip_copy("b", which, sb, rb, j, j, j).wait_send()
            relay_copy(which, j).wait_send()
            return 0

        lax.fori_loop(1, chips, body, 0)

    def apply_carries(which, reads, h):
        pt, rx, oc = scratch["pt"].at[which], scratch["rx"].at[which], scratch["oc"]
        own_user = pt[0, share + 1 : share + 2, 0:1].astype(f32)
        other_user = rx[0, share : share + 1, 0:1].astype(f32)
        own = jnp.where(user_col == own_user, own_col[:, h : h + 1], 0.0)
        other = jnp.where(user_col == other_user, other_col[:, h : h + 1], 0.0)
        base = h * pieces
        if pieces == 1:
            state, far = oc[base], rx[base, 0:share, :]
        else:
            state = jnp.concatenate([oc[base + q] for q in range(pieces)], axis=0)
            far = jnp.concatenate([rx[base + q, 0:share, :] for q in range(pieces)], axis=0)
        return own * matmul(reads, state, 1, 0) + other * matmul(reads, far, 1, 0)

    get_feat.wait()
    make_states(0, feat, keys_t)
    both_rows = jnp.concatenate([keys_t[...], reads_t[...]], axis=0).astype(f32).T.astype(bf16)
    in_rows, out_rows = both_rows[:, 0:nstate], both_rows[:, nstate:]
    scores = matmul(out_rows, keys_t[...], 1, 0)
    scores = jnp.where(row_of == column_of, 2.0 * scores, scores)
    scores = jnp.where(user_col == user_row, scores, 0.0)
    send_chip(0)
    if fused:
        for k in range(1, count_a):
            source = lax.rem(a + k, count_a)
            z_copy(source, k, source).wait_recv()
        w_y.start()
        w_x.start()

    mixw, y = scratch["mixw"], scratch["y"]
    for h in range(heads):
        spread = jnp.abs(along[:, h : h + 1] - cumulative[h : h + 1, :])
        weights = (scores * jnp.exp(-spread)).astype(bf16)
        mixw[h] = weights
        cols = slice(h * width, (h + 1) * width)
        y[:, cols] = matmul(weights, feat[:, cols], 1, 0)
    if fused:

        @pl.when(c == 0)
        def _():
            w_y.wait_recv()

        @pl.when(c == 1)
        def _():
            w_x.wait_recv()

        w_on.start()
    silu, cot, normed, grad_mixed = (
        scratch["silu"],
        scratch["cot"],
        scratch["normed"],
        scratch["grad_mixed"],
    )
    get_gate.wait()
    gates = gate[...].astype(f32)
    silu[...] = gates / (1.0 + jnp.exp(-gates))
    scan_states(0)
    get_grad.wait()
    if fused:

        @pl.when(c == 0)
        def _():
            w_x.wait_recv()

        @pl.when(c == 1)
        def _():
            w_y.wait_recv()

        w_on.wait_recv()
        w_core.start()
    relay(0)
    if fused:
        w_core.wait_recv()
        whole = full[...].reshape(inner_dim, out_dim)
    else:
        get_weight.wait()
        whole = scratch["full"][...]
    scale = norm_gain[...].astype(f32)
    cot[...] = matmul(out_grad[...], whole, 1, 1) * scale
    for h in range(heads):
        cols = slice(h * width, (h + 1) * width)
        y[:, cols] = (y[:, cols] + apply_carries(0, out_rows, h)) * silu[:, cols]
    gated = y[...]
    multiplier = lax.rsqrt(jnp.mean(gated * gated, axis=1, keepdims=True) + eps)
    back = cot[...]
    slope = jnp.mean(back * gated, axis=1, keepdims=True) * multiplier * multiplier
    grad_mixed[...] = ((back - gated * slope) * multiplier * silu[...]).astype(bf16)
    make_states(1, grad_mixed, reads_t)

    normed[...] = (y[...] * multiplier * scale).astype(bf16)
    if fused:
        part = scratch["part"]
        rss, rrs = scratch["rss"], scratch["rrs"]
        part[...] = matmul(normed[...], out_grad[...], 0, 0).astype(bf16).reshape(part.shape)
        one, two, turn, three, four = (
            scratch[name] for name in ("one", "two", "turn", "three", "four")
        )

        def r_copy(source, target, slot, peer):
            return remote(source, target, rss.at[count_a + slot], rrs.at[count_a + slot], peer)

        r_core = r_copy(part.at[:, :, :, 1 - c], one, 0, core_peer)
        r_far = r_copy(one.at[1 - x, :, 1 - b], two.at[0], 1, first_peer)
        r_near = r_copy(one.at[1 - fx, :, 1 - fb], two.at[1], 2, first_peer)
        r_on = r_copy(turn, two.at[2], 3, second_peer)
        r_core.start()
    else:
        weight_grad[...] = matmul(normed[...], out_grad[...], 0, 0)
    send_chip(1)
    if fused:
        r_core.wait_recv()
        one[...] = (one[...].astype(f32) + part[:, :, :, c].astype(f32)).astype(bf16)
        r_far.start()
        r_near.start()

    for h in range(heads):
        cols = slice(h * width, (h + 1) * width)
        y[:, cols] = matmul(mixw[h], grad_mixed[:, cols], 0, 0)
    mixed[...] = matmul(normed[...], whole, 1, 0).astype(bf16)
    scan_states(1)
    if fused:
        r_far.wait_recv()
        turn[...] = (two[0].astype(f32) + one[fx, :, fb].astype(f32)).astype(bf16)
        r_on.start()
    relay(1)
    if fused:
        r_near.wait_recv()
        r_on.wait_recv()
        three[...] = (
            two[1].astype(f32) + two[2].astype(f32) + one[x, :, b].astype(f32)
        ).astype(bf16)

        def last_copy(k, source, target, to):
            return remote(
                three.at[source],
                four.at[target],
                rss.at[k],
                rrs.at[target],
                {"ctx": to * 4 + b * 2 + c},
            )

        for k in range(1, count_a):
            to = lax.rem(a + k, count_a)
            last_copy(k, to, a, to).start()
    for h in range(heads):
        cols = slice(h * width, (h + 1) * width)
        feature_grad[:, cols] = (y[:, cols] + apply_carries(1, in_rows, h)).astype(bf16)
    finish_sends(0)
    finish_sends(1)
    if fused:
        result = three[a].astype(f32)
        for k in range(1, count_a):
            source = lax.rem(a + k, count_a)
            last_copy(k, source, source, source).wait_recv()
            result = result + four[source].astype(f32)
        weight_grad[...] = result
        for k in range(1, count_a):
            to = lax.rem(a + k, count_a)
            last_copy(k, to, a, to).wait_send()
            z_copy(a, k, to).wait_send()
        for copy in (w_y, w_x, w_on, w_core, r_core, r_far, r_near, r_on):
            copy.wait_send()


def local(
    dp,
    n,
    features,
    gate_in,
    state_in,
    state_out,
    step_size,
    decay_rate,
    user_ids,
    norm_gain,
    out_weight,
    out_grad,
):
    tokens, inner_dim = features.shape[1:]
    heads = step_size.shape[1]
    width = inner_dim // heads
    nstate = state_in.shape[2]
    rows, out_dim = out_weight.shape
    fused = dp == 2 and n == 16 and rows % 16 == 0
    share = 2 * heads * nstate // n
    chips = n // 2
    states = pltpu.VMEM((2, chips, share + AUX, width), bf16)
    dma = pltpu.SemaphoreType.DMA
    scratch = dict(
        st=pltpu.VMEM((2, 2, chips, share + AUX, width), bf16),
        pt=states,
        ct=states,
        ra=states,
        sb=states,
        rb=states,
        rx=states,
        oc=pltpu.VMEM((chips, share, width), bf16),
        p_send=dma((2,)),
        p_recv=dma((2,)),
        a_send=dma((2, chips)),
        a_recv=dma((2, chips)),
        b_send=dma((2, chips)),
        b_recv=dma((2, chips)),
        x_send=dma((2, chips)),
        x_recv=dma((2, chips)),
        loads=dma((4,)),
        feat=pltpu.VMEM((tokens, inner_dim), bf16),
        gate=pltpu.VMEM((tokens, inner_dim), bf16),
        out_grad=pltpu.VMEM((tokens, out_dim), bf16),
        mixw=pltpu.VMEM((heads, tokens, tokens), bf16),
        y=pltpu.VMEM((tokens, inner_dim), f32),
        silu=pltpu.VMEM((tokens, inner_dim), f32),
        cot=pltpu.VMEM((tokens, inner_dim), f32),
        normed=pltpu.VMEM((tokens, inner_dim), bf16),
        grad_mixed=pltpu.VMEM((tokens, inner_dim), bf16),
    )
    if fused:
        count_a = n // 4
        sems = dma((count_a + 4,))
        quarter = (count_a, rows, out_dim)
        scratch.update(
            full=pltpu.VMEM((2, count_a, 2, 2, rows, out_dim), bf16),
            part=pltpu.VMEM((2, count_a, 2, 2, rows, out_dim), bf16),
            one=pltpu.VMEM((2, count_a, 2, rows, out_dim), bf16),
            two=pltpu.VMEM((3, *quarter), bf16),
            turn=pltpu.VMEM(quarter, bf16),
            three=pltpu.VMEM(quarter, bf16),
            four=pltpu.VMEM(quarter, bf16),
            wss=sems,
            wrs=sems,
            rss=sems,
            rrs=sems,
        )
        held = out_weight
    else:
        held = lax.all_gather(out_weight, ("dp", "ctx"), axis=0, tiled=True)
        scratch.update(full=pltpu.VMEM(held.shape, bf16))
    names = list(scratch)

    def body(*refs):
        kernel(n, fused, *refs[:13], dict(zip(names, refs[13:])))

    vmem = pl.BlockSpec(memory_space=pltpu.VMEM)
    smem = pl.BlockSpec(memory_space=pltpu.SMEM)
    hbm = pl.BlockSpec(memory_space=pltpu.HBM)
    mixed, feature_grad, weight_grad = pl.pallas_call(
        body,
        out_shape=(
            jax.ShapeDtypeStruct((tokens, out_dim), bf16),
            jax.ShapeDtypeStruct((tokens, inner_dim), bf16),
            jax.ShapeDtypeStruct(held.shape, f32),
        ),
        in_specs=[hbm, hbm, vmem, vmem, vmem, smem, vmem, vmem, hbm, hbm],
        out_specs=(vmem, vmem, vmem),
        scratch_shapes=list(scratch.values()),
        compiler_params=pltpu.CompilerParams(
            collective_id=0, has_side_effects=True, vmem_limit_bytes=62 << 20
        ),
        name="mixer",
    )(
        features[0],
        gate_in[0],
        state_in[0].T,
        state_out[0].T,
        step_size[0],
        decay_rate,
        user_ids,
        norm_gain.reshape(1, -1),
        held,
        out_grad[0],
    )
    if not fused:
        weight_grad = lax.psum_scatter(
            weight_grad, ("dp", "ctx"), scatter_dimension=0, tiled=True
        )
    return mixed[None], feature_grad[None], weight_grad


def solution(mesh):
    placed = (
        P("dp", "ctx", None),
        P("dp", "ctx", None),
        P("dp", "ctx", None),
        P("dp", "ctx", None),
        P("dp", None, "ctx"),
        P(),
        P("dp", "ctx"),
        P(),
        P(("dp", "ctx"), None),
        P("dp", "ctx", None),
    )
    return jax.shard_map(
        functools.partial(local, mesh.shape["dp"], mesh.shape["ctx"]),
        mesh=mesh,
        in_specs=placed,
        out_specs=(P("dp", "ctx", None), P("dp", "ctx", None), P(("dp", "ctx"), None)),
        check_vma=False,
    )
```

time: 63.5 us -> 47.9 us (0.75)
  Pallas kernels: 55.4 us -> 42.6 us
  local copies, waits for them, and re-layouts: 7.1 us -> 4.38 us
    pallas_call x1, Pallas kernels: 55.4 us -> 42.6 us  [local(): pl.pallas_call(body, out_shape=(jax.ShapeDtypeStruct((tokens, out_dim), b...]
    unnamed x23 -> x9, local copies, waits for them, and re-layouts: 7.1 us -> 3.78 us
where the time goes in v2:
time: 47.9 us; the launch traced here: 47.7 us
  Pallas kernels  42.6 us (89%)
  local copies, waits for them, and re-layouts  4.38 us (9%)
  between operations  0.66 us (1%)
    pallas_call x1, Pallas kernels, local(): pl.pallas_call(body, out_shape=(jax.ShapeDtypeStruct((tokens, out_dim), b...  42.6 us
    unnamed x9, local copies, waits for them, and re-layouts  3.78 us

profile of v2, /device:TPU:0, one launch (start us, length us, event | category | flops | bytes accessed | tf_op | source)
XLA Modules:
  0.0 47.7 jit_solution(1268101832964446086)
XLA Ops:
  0.6 0.0 copy-start.2
  0.6 0.7 %copy-done.2 = bf16[1024]{0:T(1024)(128)(2,1)S(1)} copy-done((bf16[1024]{0:T(1024)(128)(2,1)S(1)}, bf16[1024]{0:T(1024)(128)(2,1)}, u32[]{:S(2)}) %copy-start.2) | copy-done | bytes 2072
  1.3 0.6 %reshape.9.refs_7_ = bf16[1,1024]{1,0:T(2,128)(2,1)} reshape(bf16[1024]{0:T(1024)(128)(2,1)S(1)} %copy-done.2) | data formatting | bytes 4096 | tf_op jit(solution)/shard_map/reshape | solution.py:562
  1.9 42.6 %mixer.1 = (bf16[128,512]{1,0:T(8,128)(2,1)}, bf16[128,1024]{1,0:T(8,128)(2,1)}, f32[32,512]{1,0:T(8,128)}) custom-call(bf16[128,1024]{1,0:T(8,128)(2,1)} %bitcast.12, bf16[128,1024]{1,0:T(8,128)(2,1)} %bitcast.13, bf16[64,128]{1,0:T(8,128)(2,1)} %bitcast.17, bf16[64,128]{1,0:T(8,128)(2,1)} %bitcast.18, f32[8,128]{1,0:T(8,128)} %bitcast.19, f32[8]{0:T(128)} %refs_5_.1, ...), custom_call_target="tpu_custom_call" | custom-call | tf_op jit(solution)/shard_map/mixer/pallas_call | solution.py:540
  44.6 0.0 copy-start
  44.6 1.6 %copy.16 = bf16[1,128,512]{2,1,0:T(8,128)(2,1)} copy(bf16[1,128,512]{2,1,0:T(8,128)(2,1)} %bitcast.15) | data formatting | bytes 262144
  46.2 0.0 copy-done
  46.2 0.0 copy-start.1
  46.2 0.7 %copy.17 = bf16[1,128,1024]{2,1,0:T(8,128)(2,1)} copy(bf16[1,128,1024]{2,1,0:T(8,128)(2,1)S(1)} %bitcast.14) | data formatting | bytes 524288
  46.9 0.2 copy-done.1
  47.0 0.6 %copy.18 = f32[32,512]{1,0:T(8,128)} copy(f32[32,512]{1,0:T(8,128)S(1)} %copy-done.1) | data formatting | bytes 131072
Async XLA Ops:
  0.6 0.7 %copy-start.2 = (bf16[1024]{0:T(1024)(128)(2,1)S(1)}, bf16[1024]{0:T(1024)(128)(2,1)}, u32[]{:S(2)}) copy-start(bf16[1024]{0:T(1024)(128)(2,1)} %param.17) | copy-start | bytes 6148
  44.6 1.6 %copy-start = (bf16[128,1024]{1,0:T(8,128)(2,1)S(1)}, bf16[128,1024]{1,0:T(8,128)(2,1)}, u32[]{:S(2)}) copy-start(bf16[128,1024]{1,0:T(8,128)(2,1)} %get-tuple-element.7) | copy-start | bytes 786436
  46.2 0.9 %copy-start.1 = (f32[32,512]{1,0:T(8,128)S(1)}, f32[32,512]{1,0:T(8,128)}, u32[]{:S(2)}) copy-start(f32[32,512]{1,0:T(8,128)} %get-tuple-element.14) | copy-start | bytes 196612

commit v3 on v2

--- a/solution.py
+++ b/solution.py
@@ -119,7 +119,11 @@
         w_y = w_copy(full.at[x, :, b, c], 0, y_peer)
         w_x = w_copy(full.at[x, :, b, c], 1, x_peer)
         w_on = w_copy(full.at[fx, :, fb, c], 2, first_peer)
-        w_core = w_copy(full.at[:, :, :, c], 3, core_peer)
+        quarters = ((1 - x, 1 - b), (1 - x, b), (x, 1 - b), (x, b))
+        w_core = [
+            w_copy(full.at[i, :, j, c], 3 + slot, core_peer)
+            for slot, (i, j) in enumerate(quarters)
+        ]
 
     row_of = lax.broadcasted_iota(jnp.int32, (tokens, tokens), 0)
     column_of = lax.broadcasted_iota(jnp.int32, (tokens, tokens), 1)
@@ -320,6 +324,7 @@
             z_copy(source, k, source).wait_recv()
         w_y.start()
         w_x.start()
+        w_core[3].start()
 
     mixw, y = scratch["mixw"], scratch["y"]
     for h in range(heads):
@@ -333,12 +338,15 @@
         @pl.when(c == 0)
         def _():
             w_y.wait_recv()
+            w_on.start()
+            w_core[2].start()
 
         @pl.when(c == 1)
         def _():
             w_x.wait_recv()
-
-        w_on.start()
+            w_on.start()
+            w_core[1].start()
+
     silu, cot, normed, grad_mixed = (
         scratch["silu"],
         scratch["cot"],
@@ -355,21 +363,24 @@
         @pl.when(c == 0)
         def _():
             w_x.wait_recv()
+            w_core[1].start()
 
         @pl.when(c == 1)
         def _():
             w_y.wait_recv()
+            w_core[2].start()
 
         w_on.wait_recv()
-        w_core.start()
+        w_core[0].start()
     relay(0)
     if fused:
-        w_core.wait_recv()
+        for copy in w_core:
+            copy.wait_recv()
         whole = full[...].reshape(inner_dim, out_dim)
     else:
         get_weight.wait()
         whole = scratch["full"][...]
-    scale = norm_gain[...].astype(f32)
+    scale = norm_gain[...].astype(f32).reshape(1, -1)
     cot[...] = matmul(out_grad[...], whole, 1, 1) * scale
     for h in range(heads):
         cols = slice(h * width, (h + 1) * width)
@@ -393,19 +404,26 @@
         def r_copy(source, target, slot, peer):
             return remote(source, target, rss.at[count_a + slot], rrs.at[count_a + slot], peer)
 
-        r_core = r_copy(part.at[:, :, :, 1 - c], one, 0, core_peer)
-        r_far = r_copy(one.at[1 - x, :, 1 - b], two.at[0], 1, first_peer)
-        r_near = r_copy(one.at[1 - fx, :, 1 - fb], two.at[1], 2, first_peer)
-        r_on = r_copy(turn, two.at[2], 3, second_peer)
-        r_core.start()
+        r_core = [
+            r_copy(part.at[i, :, j, 1 - c], one.at[i, :, j], slot, core_peer)
+            for slot, (i, j) in enumerate(quarters)
+        ]
+        r_far = r_copy(one.at[1 - x, :, 1 - b], two.at[0], 4, first_peer)
+        r_near = r_copy(one.at[1 - fx, :, 1 - fb], two.at[1], 5, first_peer)
+        r_on = r_copy(turn, two.at[2], 6, second_peer)
+        for copy in r_core:
+            copy.start()
     else:
         weight_grad[...] = matmul(normed[...], out_grad[...], 0, 0)
     send_chip(1)
     if fused:
-        r_core.wait_recv()
-        one[...] = (one[...].astype(f32) + part[:, :, :, c].astype(f32)).astype(bf16)
-        r_far.start()
-        r_near.start()
+        for slot, (i, j) in enumerate(quarters):
+            r_core[slot].wait_recv()
+            one[i, :, j] = (one[i, :, j].astype(f32) + part[i, :, j, c].astype(f32)).astype(bf16)
+            if slot == 0:
+                r_far.start()
+            if slot == 2:
+                r_near.start()
 
     for h in range(heads):
         cols = slice(h * width, (h + 1) * width)
@@ -452,7 +470,7 @@
             to = lax.rem(a + k, count_a)
             last_copy(k, to, a, to).wait_send()
             z_copy(a, k, to).wait_send()
-        for copy in (w_y, w_x, w_on, w_core, r_core, r_far, r_near, r_on):
+        for copy in (w_y, w_x, w_on, r_far, r_near, r_on, *w_core, *r_core):
             copy.wait_send()
 
 
@@ -510,7 +528,7 @@
     )
     if fused:
         count_a = n // 4
-        sems = dma((count_a + 4,))
+        sems = dma((count_a + 7,))
         quarter = (count_a, rows, out_dim)
         scratch.update(
             full=pltpu.VMEM((2, count_a, 2, 2, rows, out_dim), bf16),
@@ -559,7 +577,7 @@
         step_size[0],
         decay_rate,
         user_ids,
-        norm_gain.reshape(1, -1),
+        norm_gain,
         held,
         out_grad[0],
     )

time: 47.9 us -> 46.8 us (0.977)
  local copies, waits for them, and re-layouts: 4.38 us -> 3.11 us
    unnamed x9 -> x7, local copies, waits for them, and re-layouts: 3.78 us -> 3.11 us
    reshape x1 -> x0, local copies, waits for them, and re-layouts: 0.6 us -> none  [local(): norm_gain.reshape(1, -1)]
where the time goes in v3:
time: 46.8 us; the launch traced here: 46.6 us
  Pallas kernels  42.9 us (92%)
  local copies, waits for them, and re-layouts  3.11 us (7%)
  between operations  0.65 us (1%)
    pallas_call x1, Pallas kernels, local(): pl.pallas_call(body, out_shape=(jax.ShapeDtypeStruct((tokens, out_dim), b...  42.9 us
    unnamed x7, local copies, waits for them, and re-layouts  3.11 us

profile of v3, /device:TPU:0, one launch (start us, length us, event | category | flops | bytes accessed | tf_op | source)
XLA Modules:
  0.0 46.6 jit_solution(12526358289337494976)
XLA Ops:
  0.6 42.9 %mixer.1 = (bf16[128,512]{1,0:T(8,128)(2,1)}, bf16[128,1024]{1,0:T(8,128)(2,1)}, f32[32,512]{1,0:T(8,128)}) custom-call(bf16[128,1024]{1,0:T(8,128)(2,1)} %bitcast.12, bf16[128,1024]{1,0:T(8,128)(2,1)} %bitcast.13, bf16[64,128]{1,0:T(8,128)(2,1)} %bitcast.17, bf16[64,128]{1,0:T(8,128)(2,1)} %bitcast.18, f32[8,128]{1,0:T(8,128)} %bitcast.19, f32[8]{0:T(128)} %refs_5_.1, ...), custom_call_target="tpu_custom_call" | custom-call | tf_op jit(solution)/shard_map/mixer/pallas_call | solution.py:558
  43.5 0.0 copy-start
  43.5 1.6 %copy.16 = bf16[1,128,512]{2,1,0:T(8,128)(2,1)} copy(bf16[1,128,512]{2,1,0:T(8,128)(2,1)} %bitcast.15) | data formatting | bytes 262144
  45.1 0.0 copy-done
  45.1 0.0 copy-start.1
  45.1 0.7 %copy.17 = bf16[1,128,1024]{2,1,0:T(8,128)(2,1)} copy(bf16[1,128,1024]{2,1,0:T(8,128)(2,1)S(1)} %bitcast.14) | data formatting | bytes 524288
  45.8 0.2 copy-done.1
  46.0 0.6 %copy.18 = f32[32,512]{1,0:T(8,128)} copy(f32[32,512]{1,0:T(8,128)S(1)} %copy-done.1) | data formatting | bytes 131072
Async XLA Ops:
  43.5 1.6 %copy-start = (bf16[128,1024]{1,0:T(8,128)(2,1)S(1)}, bf16[128,1024]{1,0:T(8,128)(2,1)}, u32[]{:S(2)}) copy-start(bf16[128,1024]{1,0:T(8,128)(2,1)} %get-tuple-element.7) | copy-start | bytes 786436
  45.1 0.9 %copy-start.1 = (f32[32,512]{1,0:T(8,128)S(1)}, f32[32,512]{1,0:T(8,128)}, u32[]{:S(2)}) copy-start(f32[32,512]{1,0:T(8,128)} %get-tuple-element.14) | copy-start | bytes 196612
